TPU v7x, 32 devices: a whole 2x2x4 slice. The times are simulated.
32 devices in a mesh: groups: 2 (over x), img: 16 (over z, y, core).
Axes of the slice: x: 2, y: 2, z: 4, core: 2. Of those that a mesh axis runs over, the one named last changes fastest.
Arguments:
- caches: bfloat16 [32, 768, 1024], P(('groups', 'img')), parts along dimension 0, may hold values from -170 to 170
- owner_slot: int32 [32], P('groups'), parts along dimension 0, may hold values from 0 to 15, each once
- pairs: int32 [32, 2], P('groups'), parts along dimension 0, may hold values from 0 to 15, as said below
- block_mask: int32 [32, 12, 12], P(('groups', 'img')), parts along dimension 0, may hold values from 0 to 1, as said below
- cotangent: bfloat16 [32, 768, 768], P(('groups', 'img')), parts along dimension 0, may hold values from -6 to 6
- embed_weight: bfloat16 [1024, 768], replicated, may hold values from -0.1875 to 0.1875
- query_weight: bfloat16 [768, 512], replicated, may hold values from -2 to 2
- key_weight: bfloat16 [768, 512], replicated, may hold values from -2 to 2
- value_weight: bfloat16 [768, 512], replicated, may hold values from -0.21875 to 0.21875
- out_weight: bfloat16 [768, 512], replicated, may hold values from -0.25 to 0.25
Outputs:
- attended: bfloat16 [32, 768, 768], P(('groups', 'img')), parts along dimension 0
- gradients: float32 [1536, 2048], P(('groups', 'img')), parts along dimension 0
There are 2 independent parts, one for each index of `groups`. A program takes and returns all parts, laid end to end along the dimension named above; an argument that names none is the same for every part. Nothing has to cross between parts.
Inputs may be any that keep to these rules, and one draw needn't show every extreme that they name: `pairs`: each row names two different images. `block_mask`: block (i, i) is live in every pair.
All inputs are finite; a program needn't handle non-finite values.
Results may differ from a plain program's by a relative error of at most 0.012.
Values may be sent and summed in bfloat16 or wider, within the bound.
No kernel may reach another device: no remote copies, remote signals or barrier semaphores. Data moves between devices by JAX's collectives and lax.ppermute only.
A program may use at most 128 MiB of HBM per device.

v0:
```python
import math
import jax
import jax.numpy as jnp
from jax import lax
from jax.sharding import PartitionSpec as P

HEADS = 8
BLOCK = 64


def layer_normed(tokens):
    values_f = tokens.astype(jnp.float32)
    centred = values_f - jnp.mean(values_f, axis=-1, keepdims=True)
    spread_sq = jnp.mean(centred * centred, axis=-1, keepdims=True)
    return (centred * lax.rsqrt(spread_sq + 1e-06)).astype(jnp.bfloat16)


def split_heads(matrix, heads):
    length, width = matrix.shape
    return matrix.reshape(length, heads, width // heads).transpose(1, 0, 2)


def merge_heads(stacked):
    heads, length, hsize = stacked.shape
    return stacked.transpose(1, 0, 2).reshape(length, heads * hsize)


def pair_pass(
    query_tokens,
    key_tokens,
    mask_blocks,
    cotangent,
    query_weight,
    key_weight,
    value_weight,
    out_weight,
    heads,
    block,
):
    query_normed = layer_normed(query_tokens)
    key_normed = layer_normed(key_tokens)
    queries = jnp.dot(query_normed, query_weight, preferred_element_type=jnp.float32).astype(
        jnp.bfloat16
    )
    keys_all = jnp.dot(key_normed, key_weight, preferred_element_type=jnp.float32).astype(
        jnp.bfloat16
    )
    values_all = jnp.dot(key_normed, value_weight, preferred_element_type=jnp.float32).astype(
        jnp.bfloat16
    )
    grad_context = jnp.dot(cotangent, out_weight, preferred_element_type=jnp.float32).astype(
        jnp.bfloat16
    )
    live_mask = jnp.repeat(jnp.repeat(mask_blocks, block, axis=0), block, axis=1) > 0
    scaling = 1.0 / math.sqrt(queries.shape[1] // heads)

    def one_head(operands):
        head_query, head_key, head_value, head_grad = operands
        scores = jnp.dot(head_query, head_key.T, preferred_element_type=jnp.float32) * scaling
        masked = jnp.where(live_mask, scores, -jnp.inf)
        row_max = jnp.max(masked, axis=1, keepdims=True)
        weights = jnp.exp(masked - row_max)
        probability = weights / jnp.sum(weights, axis=1, keepdims=True)
        probability_low = probability.astype(jnp.bfloat16)
        context = jnp.dot(probability_low, head_value, preferred_element_type=jnp.float32).astype(
            jnp.bfloat16
        )
        grad_value = jnp.dot(
            probability_low.T, head_grad, preferred_element_type=jnp.float32
        ).astype(jnp.bfloat16)
        grad_prob = jnp.dot(head_grad, head_value.T, preferred_element_type=jnp.float32)
        inner_sum = jnp.sum(probability * grad_prob, axis=1, keepdims=True)
        grad_score = (probability * (grad_prob - inner_sum) * scaling).astype(jnp.bfloat16)
        grad_query = jnp.dot(grad_score, head_key, preferred_element_type=jnp.float32).astype(
            jnp.bfloat16
        )
        grad_key = jnp.dot(grad_score.T, head_query, preferred_element_type=jnp.float32).astype(
            jnp.bfloat16
        )
        return (context, grad_value, grad_query, grad_key)

    stacked = lax.map(
        one_head,
        (
            split_heads(queries, heads),
            split_heads(keys_all, heads),
            split_heads(values_all, heads),
            split_heads(grad_context, heads),
        ),
    )
    context, grad_value, grad_query, grad_key = [merge_heads(member) for member in stacked]
    attended = (
        query_tokens.astype(jnp.float32)
        + jnp.dot(context, out_weight.T, preferred_element_type=jnp.float32)
    ).astype(jnp.bfloat16)
    return (
        attended,
        (query_normed, key_normed, grad_query, grad_key, grad_value, cotangent, context),
    )


def gradient_rows(kept):
    query_normed, key_normed, grad_query, grad_key, grad_value, cotangent, context = kept
    return jnp.concatenate(
        [
            jnp.dot(query_normed.T, grad_query, preferred_element_type=jnp.float32),
            jnp.dot(key_normed.T, grad_key, preferred_element_type=jnp.float32),
            jnp.dot(key_normed.T, grad_value, preferred_element_type=jnp.float32),
            jnp.dot(cotangent.T, context, preferred_element_type=jnp.float32),
        ],
        axis=1,
    )


def embedded_of(tokens, embed_weight):
    shape_in = tokens.shape
    flat = tokens.reshape(-1, shape_in[-1])
    product = jnp.dot(flat, embed_weight, preferred_element_type=jnp.float32).astype(jnp.bfloat16)
    return product.reshape(shape_in[:-1] + (embed_weight.shape[1],))


def per_device(
    caches,
    owner_slot,
    pairs,
    block_mask,
    cotangent,
    embed_weight,
    query_weight,
    key_weight,
    value_weight,
    out_weight,
):
    devices_img = lax.axis_size("img")
    images_here = caches.shape[0]
    length = caches.shape[1]
    pairs_here = block_mask.shape[0]
    width = caches.shape[-1]
    portion = length // devices_img
    pieces = caches.reshape(images_here, devices_img, portion, width)
    spread = lax.all_to_all(pieces, "img", split_axis=1, concat_axis=0, tiled=True)
    table = spread.reshape(images_here * devices_img, portion, width)
    slots = owner_slot[pairs].reshape(devices_img, pairs_here, 2).transpose(1, 2, 0)
    picked = table[slots]
    arrived = lax.all_to_all(picked, "img", split_axis=2, concat_axis=3, tiled=True)
    tokens = arrived.reshape(pairs_here, 2, length, width)
    tokens = embedded_of(tokens, embed_weight)
    attended, kept = pair_pass(
        tokens[0, 0],
        tokens[0, 1],
        block_mask[0],
        cotangent[0],
        query_weight,
        key_weight,
        value_weight,
        out_weight,
        HEADS,
        BLOCK,
    )
    attended_list = [attended]
    attended_all = jnp.stack(attended_list)
    inverse = 1.0 / (pairs_here * devices_img)
    total = gradient_rows(kept)
    summed = lax.psum_scatter(total, "img", scatter_dimension=0, tiled=True)
    return (attended_all, summed * inverse)


def solution(mesh):
    placed = (
        P(("groups", "img"), None, None),
        P("groups"),
        P("groups", None),
        P(("groups", "img"), None, None),
        P(("groups", "img"), None, None),
        P(),
        P(),
        P(),
        P(),
        P(),
    )
    return jax.shard_map(
        per_device,
        mesh=mesh,
        in_specs=placed,
        out_specs=(P(("groups", "img"), None, None), P(("groups", "img"), None)),
        check_vma=False,
    )
```

profile of v0, /device:TPU:0, one launch (start us, length us, event | category | flops | bytes accessed | tf_op | source)
XLA Modules:
  0.0 350.0 jit_solution(1653082750887615736)
XLA Ops:
  7.2 7.5 %all-to-all-start = ((bf16[1,16,48,1024]{3,2,0,1:T(8,128)(2,1)}), bf16[1,16,48,1024]{3,2,0,1:T(8,128)(2,1)S(1)}, u32[]{:S(2)}, u32[]{:S(2)}) async-start(bf16[1,16,48,1024]{3,2,0,1:T(8,128)(2,1)} %bitcast.197), calls=%async_computation | async-start | bytes 3145728 | tf_op jit(solution)/shard_map/all_to_all | solution.py:141
  15.9 30.8 %all-to-all-done = bf16[1,16,48,1024]{3,2,0,1:T(8,128)(2,1)S(1)} async-done(((bf16[1,16,48,1024]{3,2,0,1:T(8,128)(2,1)}), bf16[1,16,48,1024]{3,2,0,1:T(8,128)(2,1)S(1)}, u32[]{:S(2)}, u32[]{:S(2)}) %all-to-all-start) | async-done | bytes 1572896 | tf_op jit(solution)/shard_map/all_to_all | solution.py:141
  46.7 2.4 gather_fusion.1
  49.1 4.0 %copy.39 = bf16[1,2,16,48,1024]{4,3,1,0,2:T(8,128)(2,1)} copy(bf16[1,2,16,48,1024]{4,3,2,1,0:T(8,128)(2,1)} %bitcast.182) | data formatting | bytes 6291456 | tf_op jit(solution)/shard_map/gather | solution.py:144
  53.2 9.3 %all-to-all-start.1 = ((bf16[1,2,16,48,1024]{4,3,1,0,2:T(8,128)(2,1)}), bf16[1,2,16,48,1024]{4,3,1,0,2:T(8,128)(2,1)}, u32[]{:S(2)}, u32[]{:S(2)}) async-start(bf16[1,2,16,48,1024]{4,3,1,0,2:T(8,128)(2,1)} %copy.39), calls=%async_computation.1 | async-start | bytes 6291456 | tf_op jit(solution)/shard_map/all_to_all | solution.py:145
  62.6 2.0 convolution_convert_fusion.5
  66.4 55.5 %all-to-all-done.1 = bf16[1,2,16,48,1024]{4,3,1,0,2:T(8,128)(2,1)} async-done(((bf16[1,2,16,48,1024]{4,3,1,0,2:T(8,128)(2,1)}), bf16[1,2,16,48,1024]{4,3,1,0,2:T(8,128)(2,1)}, u32[]{:S(2)}, u32[]{:S(2)}) %all-to-all-start.1) | async-done | bytes 3145760 | tf_op jit(solution)/shard_map/all_to_all | solution.py:145
  121.9 2.4 copy.40
  124.3 2.8 convolution_convert_fusion.4
  131.5 2.3 convolution_convert_fusion.7
  134.7 3.4 convolution_convert_fusion.8
  139.8 85.0 %while.17 = (s32[]{:T(128)}, bf16[8,768,64]{1,2,0:T(8,128)(2,1)}, bf16[8,768,64]{1,2,0:T(8,128)(2,1)}, bf16[8,768,64]{1,2,0:T(8,128)(2,1)}, bf16[8,768,64]{1,2,0...) while((s32[]{:T(128)}, bf16[8,768,64]{1,2,0:T(8,128)(2,1)}, ...), condition=%wide.region_8.9_spmd.clone, body=%wide.region_4.8_spmd.clone.sunk | while | flops 464385792 | bytes 33088676 | solution.py:82
  143.2 2.1 fusion.117
  146.3 2.2 fusion.115
  148.5 2.0 fusion.114
  151.7 1.8 multiply_reduce_fusion.2
  153.8 2.1 fusion.117
  156.9 2.2 fusion.115
  159.2 2.0 fusion.114
  162.3 1.8 multiply_reduce_fusion.2
  164.5 2.1 fusion.117
  167.6 2.2 fusion.115
  169.8 2.0 fusion.114
  175.1 2.1 fusion.117
  178.2 2.2 fusion.115
  180.4 1.9 fusion.114
  183.5 1.8 multiply_reduce_fusion.2
  185.7 2.1 fusion.117
  188.8 2.2 fusion.115
  191.0 1.9 fusion.114
  194.1 1.8 multiply_reduce_fusion.2
  196.3 2.1 fusion.117
  199.4 2.2 fusion.115
  201.6 1.9 fusion.114
  206.9 2.1 fusion.117
  210.1 2.2 fusion.115
  212.3 2.0 fusion.114
  217.6 2.1 fusion.117
  220.7 2.2 fusion.115
  222.9 2.0 fusion.114
  224.8 2.6 fusion.58
  228.5 2.2 fusion.73
  230.7 1.9 convolution_bitcast_fusion
  232.6 3.1 pad_maximum_fusion
  235.7 6.6 %copy.48 = f32[768,2048]{1,0:T(8,128)} copy(f32[768,2048]{0,1:T(8,128)} %pad_maximum_fusion) | data formatting | bytes 12582912
  243.5 3.5 fusion.55
  246.9 91.5 %reduce-scatter.4.cloned.1.call-done = f32[48,2048]{1,0:T(8,128)} async-done(((f32[768,2048]{1,0:T(8,128)}), f32[48,2048]{1,0:T(8,128)}) %reduce-scatter.4.cloned.1.call-update) | async-done | bytes 393232
  340.9 2.3 copy.46
  (127 shorter events, 42.0 us)
Async XLA Ops:
  7.2 117.1 %copy-start = (bf16[1024,768]{1,0:T(8,128)(2,1)S(1)}, bf16[1024,768]{1,0:T(8,128)(2,1)}, u32[]{:S(2)}) copy-start(bf16[1024,768]{1,0:T(8,128)(2,1)} %param.17) | copy-start | bytes 4718596
  7.2 7.6 %copy-start.8 = (s32[16,2]{0,1:T(2,128)S(1)}, s32[16,2]{0,1:T(2,128)}, u32[]{:S(2)}) copy-start(s32[16,2]{0,1:T(2,128)} %param.14) | copy-start | bytes 388
  7.2 7.8 %copy-start.2 = (s32[16]{0:T(128)S(1)}, s32[16]{0:T(128)}, u32[]{:S(2)}) copy-start(s32[16]{0:T(128)} %param.13) | copy-start | bytes 196
  7.2 39.5 %all-to-all-start = ((bf16[1,16,48,1024]{3,2,0,1:T(8,128)(2,1)}), bf16[1,16,48,1024]{3,2,0,1:T(8,128)(2,1)S(1)}, u32[]{:S(2)}, u32[]{:S(2)}) async-start(bf16[1,16,48,1024]{3,2,0,1:T(8,128)(2,1)} %bitcast.197), calls=%async_computation | async-start | bytes 3145728 | tf_op jit(solution)/shard_map/all_to_all | solution.py:141
  53.2 9.4 %copy-start.9 = (bf16[1,768,768]{2,1,0:T(8,128)(2,1)S(1)}, bf16[1,768,768]{2,1,0:T(8,128)(2,1)}, u32[]{:S(2)}) copy-start(bf16[1,768,768]{2,1,0:T(8,128)(2,1)} %param.16) | copy-start | bytes 3538948
  53.2 68.7 %all-to-all-start.1 = ((bf16[1,2,16,48,1024]{4,3,1,0,2:T(8,128)(2,1)}), bf16[1,2,16,48,1024]{4,3,1,0,2:T(8,128)(2,1)}, u32[]{:S(2)}, u32[]{:S(2)}) async-start(bf16[1,2,16,48,1024]{4,3,1,0,2:T(8,128)(2,1)} %copy.39), calls=%async_computation.1 | async-start | bytes 6291456 | tf_op jit(solution)/shard_map/all_to_all | solution.py:145
  62.5 276.0 %reduce-scatter.4.cloned.1.call-start = ((), (), s32[]{:S(2)}) async-start(), calls=%async_computation.3 | async-start | bytes 6684672
  62.6 3.5 %copy-start.7 = (s32[1,12,12]{2,0,1:T(1,128)S(1)}, s32[1,12,12]{2,0,1:T(1,128)}, u32[]{:S(2)}) copy-start(s32[1,12,12]{2,0,1:T(1,128)} %param.15) | copy-start | bytes 1732
  127.1 1.4 copy-start.3
  127.1 1.7 copy-start.11
  129.9 1.6 copy-start.12
  139.8 1.2 copy-start.5
  146.3 4.2 %copy-start.6 = (bf16[8,768,64]{2,1,0:T(8,128)(2,1)S(1)}, bf16[8,768,64]{2,1,0:T(8,128)(2,1)}, u32[]{:S(2)}) copy-start(bf16[8,768,64]{2,1,0:T(8,128)(2,1)} %copy-done.5) | copy-start | bytes 2359300 | tf_op jit(solution)/shard_map/while
  150.5 1.2 copy-start.5
  156.9 4.2 %copy-start.6 = (bf16[8,768,64]{2,1,0:T(8,128)(2,1)S(1)}, bf16[8,768,64]{2,1,0:T(8,128)(2,1)}, u32[]{:S(2)}) copy-start(bf16[8,768,64]{2,1,0:T(8,128)(2,1)} %copy-done.5) | copy-start | bytes 2359300 | tf_op jit(solution)/shard_map/while
  161.1 1.2 copy-start.5
  167.6 4.2 %copy-start.6 = (bf16[8,768,64]{2,1,0:T(8,128)(2,1)S(1)}, bf16[8,768,64]{2,1,0:T(8,128)(2,1)}, u32[]{:S(2)}) copy-start(bf16[8,768,64]{2,1,0:T(8,128)(2,1)} %copy-done.5) | copy-start | bytes 2359300 | tf_op jit(solution)/shard_map/while
  171.7 1.2 copy-start.5
  178.2 4.2 %copy-start.6 = (bf16[8,768,64]{2,1,0:T(8,128)(2,1)S(1)}, bf16[8,768,64]{2,1,0:T(8,128)(2,1)}, u32[]{:S(2)}) copy-start(bf16[8,768,64]{2,1,0:T(8,128)(2,1)} %copy-done.5) | copy-start | bytes 2359300 | tf_op jit(solution)/shard_map/while
  182.4 1.2 copy-start.5
  188.8 4.2 %copy-start.6 = (bf16[8,768,64]{2,1,0:T(8,128)(2,1)S(1)}, bf16[8,768,64]{2,1,0:T(8,128)(2,1)}, u32[]{:S(2)}) copy-start(bf16[8,768,64]{2,1,0:T(8,128)(2,1)} %copy-done.5) | copy-start | bytes 2359300 | tf_op jit(solution)/shard_map/while
  193.0 1.2 copy-start.5
  199.4 4.2 %copy-start.6 = (bf16[8,768,64]{2,1,0:T(8,128)(2,1)S(1)}, bf16[8,768,64]{2,1,0:T(8,128)(2,1)}, u32[]{:S(2)}) copy-start(bf16[8,768,64]{2,1,0:T(8,128)(2,1)} %copy-done.5) | copy-start | bytes 2359300 | tf_op jit(solution)/shard_map/while
  203.6 1.2 copy-start.5
  210.1 4.2 %copy-start.6 = (bf16[8,768,64]{2,1,0:T(8,128)(2,1)S(1)}, bf16[8,768,64]{2,1,0:T(8,128)(2,1)}, u32[]{:S(2)}) copy-start(bf16[8,768,64]{2,1,0:T(8,128)(2,1)} %copy-done.5) | copy-start | bytes 2359300 | tf_op jit(solution)/shard_map/while
  214.2 1.2 copy-start.5
  220.7 4.2 %copy-start.6 = (bf16[8,768,64]{2,1,0:T(8,128)(2,1)S(1)}, bf16[8,768,64]{2,1,0:T(8,128)(2,1)}, u32[]{:S(2)}) copy-start(bf16[8,768,64]{2,1,0:T(8,128)(2,1)} %copy-done.5) | copy-start | bytes 2359300 | tf_op jit(solution)/shard_map/while
  224.8 2.6 copy-start.4
  224.8 2.6 copy-start.14
  228.5 2.2 copy-start.10
  242.3 1.1 copy-start.13
  243.5 99.7 %copy-start.1 = (bf16[1024,768]{1,0:T(8,128)(2,1)S(1)}, bf16[1024,768]{1,0:T(8,128)(2,1)}, u32[]{:S(2)}) copy-start(bf16[1024,768]{1,0:T(8,128)(2,1)} %param.17) | copy-start | bytes 4718596
Sparse Core Ops, SparseCore 0:
  242.5 95.9 reduce-scatter.3
where the time goes:
time: 351 us; the launch traced here: 350 us
  waiting for transfers between devices  178 us (51%)
  matrix products  99.2 us (28%)
  local copies, waits for them, and re-layouts  29.2 us (8%)
  starting transfers between devices  16.9 us (5%)
  between operations  14.4 us (4%)
  other arithmetic  12.4 us (4%)
    unnamed x2, waiting for transfers between devices  91.6 us
    all_to_all x1, waiting for transfers between devices, per_device(): lax.all_to_all(picked, 'img', split_axis=2, concat_axis=3, tiled=True)  55.5 us
    all_to_all x1, waiting for transfers between devices, per_device(): lax.all_to_all(pieces, 'img', split_axis=1, concat_axis=0, tiled=True)  30.8 us
    dot_general x8, matrix products, one_head(): jnp.dot(probability_low.T, head_grad, preferred_element_type=jnp.float32)  17.7 us
    dot_general x8, matrix products, one_head(): jnp.dot(grad_score.T, head_query, preferred_element_type=jnp.float32)  16.7 us
    dot_general x8, matrix products, one_head(): jnp.dot(probability_low, head_value, preferred_element_type=jnp.float32)  15.6 us
    dot_general x8, matrix products, one_head(): jnp.dot(head_grad, head_value.T, preferred_element_type=jnp.float32)  14.5 us
    unnamed x29, local copies, waits for them, and re-layouts  11.8 us
  transfers between devices with their start and end apart: 3, of which 3 were waited for; matrix products, arithmetic and copies ran while one was open for 2% of the time, Pallas kernels for 0%

commit v1 on v0

--- a/solution.py
+++ b/solution.py
@@ -138,7 +138,10 @@
     width = caches.shape[-1]
     portion = length // devices_img
     pieces = caches.reshape(images_here, devices_img, portion, width)
-    spread = lax.all_to_all(pieces, "img", split_axis=1, concat_axis=0, tiled=True)
+    spread = jnp.concatenate(
+        lax.all_to_all(jnp.stack(jnp.split(pieces, lax.axis_size("img"), axis=1)), "img", 0, 0),
+        axis=0,
+    )
     table = spread.reshape(images_here * devices_img, portion, width)
     slots = owner_slot[pairs].reshape(devices_img, pairs_here, 2).transpose(1, 2, 0)
     picked = table[slots]

time: 351 us -> 369 us (1.051)
  local copies, waits for them, and re-layouts: 29.2 us -> 47 us
    unnamed x29 -> x46, local copies, waits for them, and re-layouts: 11.8 us -> 29 us
where the time goes in v1:
time: 369 us; the launch traced here: 367 us
  waiting for transfers between devices  178 us (48%)
  matrix products  98.9 us (27%)
  local copies, waits for them, and re-layouts  47 us (13%)
  starting transfers between devices  16.8 us (5%)
  between operations  14.4 us (4%)
  other arithmetic  12.3 us (3%)
    unnamed x2, waiting for transfers between devices  91.7 us
    all_to_all x1, waiting for transfers between devices, per_device(): lax.all_to_all(picked, 'img', split_axis=2, concat_axis=3, tiled=True)  55.5 us
    all_to_all x1, waiting for transfers between devices, per_device(): lax.all_to_all(jnp.stack(jnp.split(pieces, lax.axis_size('img'), axis=1))...  30.8 us
    unnamed x46, local copies, waits for them, and re-layouts  29 us
    dot_general x8, matrix products, one_head(): jnp.dot(probability_low.T, head_grad, preferred_element_type=jnp.float32)  16.7 us
    dot_general x8, matrix products, one_head(): jnp.dot(grad_score.T, head_query, preferred_element_type=jnp.float32)  16.6 us
    dot_general x8, matrix products, one_head(): jnp.dot(probability_low, head_value, preferred_element_type=jnp.float32)  16.5 us
    dot_general x8, matrix products, one_head(): jnp.dot(head_grad, head_value.T, preferred_element_type=jnp.float32)  14.5 us
  transfers between devices with their start and end apart: 3, of which 3 were waited for; matrix products, arithmetic and copies ran while one was open for 2% of the time, Pallas kernels for 0%

profile of v1, /device:TPU:0, one launch (start us, length us, event | category | flops | bytes accessed | tf_op | source)
XLA Modules:
  0.0 367.5 jit_solution(12697662056422691002)
XLA Ops:
  24.7 7.5 %all-to-all-start = ((bf16[16,1,1,48,1024]{4,3,2,1,0:T(8,128)(2,1)}), bf16[16,1,1,48,1024]{4,3,2,1,0:T(8,128)(2,1)S(1)}, u32[]{:S(2)}, u32[]{:S(2)}) async-start(bf16[16,1,1,48,1024]{4,3,2,1,0:T(8,128)(2,1)} %fusion.69), calls=%async_computation | async-start | bytes 3145728 | tf_op jit(solution)/shard_map/all_to_all | solution.py:142
  33.4 30.8 %all-to-all-done = bf16[16,1,1,48,1024]{4,3,2,1,0:T(8,128)(2,1)S(1)} async-done(((bf16[16,1,1,48,1024]{4,3,2,1,0:T(8,128)(2,1)}), bf16[16,1,1,48,1024]{4,3,2,1,0:T(8,128)(2,1)S(1)}, u32[]{:S(2)}, u32[]{:S(2)}) %all-to-all-start) | async-done | bytes 1572896 | tf_op jit(solution)/shard_map/all_to_all | solution.py:142
  64.2 2.4 gather_fusion.1
  66.6 4.0 %copy.38 = bf16[1,2,16,48,1024]{4,3,1,0,2:T(8,128)(2,1)} copy(bf16[1,2,16,48,1024]{4,3,2,1,0:T(8,128)(2,1)} %bitcast.246) | data formatting | bytes 6291456 | tf_op jit(solution)/shard_map/gather | solution.py:147
  70.7 9.3 %all-to-all-start.1 = ((bf16[1,2,16,48,1024]{4,3,1,0,2:T(8,128)(2,1)}), bf16[1,2,16,48,1024]{4,3,1,0,2:T(8,128)(2,1)}, u32[]{:S(2)}, u32[]{:S(2)}) async-start(bf16[1,2,16,48,1024]{4,3,1,0,2:T(8,128)(2,1)} %copy.38), calls=%async_computation.1 | async-start | bytes 6291456 | tf_op jit(solution)/shard_map/all_to_all | solution.py:148
  80.1 2.0 convolution_convert_fusion.5
  83.9 55.5 %all-to-all-done.1 = bf16[1,2,16,48,1024]{4,3,1,0,2:T(8,128)(2,1)} async-done(((bf16[1,2,16,48,1024]{4,3,1,0,2:T(8,128)(2,1)}), bf16[1,2,16,48,1024]{4,3,1,0,2:T(8,128)(2,1)}, u32[]{:S(2)}, u32[]{:S(2)}) %all-to-all-start.1) | async-done | bytes 3145760 | tf_op jit(solution)/shard_map/all_to_all | solution.py:148
  139.4 2.4 copy.39
  141.8 2.8 convolution_convert_fusion.4
  149.3 2.3 convolution_convert_fusion.7
  152.5 3.4 convolution_convert_fusion.8
  157.6 84.8 %while.17 = (s32[]{:T(128)}, bf16[8,768,64]{1,2,0:T(8,128)(2,1)}, bf16[8,768,64]{1,2,0:T(8,128)(2,1)}, bf16[8,768,64]{1,2,0:T(8,128)(2,1)}, bf16[8,768,64]{1,2,0...) while((s32[]{:T(128)}, bf16[8,768,64]{1,2,0:T(8,128)(2,1)}, ...), condition=%wide.region_8.9_spmd.clone, body=%wide.region_4.8_spmd.clone.sunk | while | flops 464385792 | bytes 33088676 | solution.py:82
  158.8 1.8 multiply_reduce_fusion.2
  161.0 2.1 fusion.133
  164.1 2.1 fusion.131
  166.2 2.1 fusion.130
  171.6 2.1 fusion.133
  174.7 2.1 fusion.131
  176.8 2.1 fusion.130
  180.0 1.8 multiply_reduce_fusion.2
  182.2 2.1 fusion.133
  185.3 2.1 fusion.131
  187.4 2.1 fusion.130
  190.6 1.8 multiply_reduce_fusion.2
  192.8 2.1 fusion.133
  195.9 2.1 fusion.131
  198.0 2.1 fusion.130
  203.4 2.1 fusion.133
  206.5 2.1 fusion.131
  208.6 2.1 fusion.130
  214.0 2.1 fusion.133
  217.1 2.1 fusion.131
  219.2 2.1 fusion.130
  222.4 1.8 multiply_reduce_fusion.2
  224.6 2.1 fusion.133
  227.7 2.1 fusion.131
  229.8 2.1 fusion.130
  235.2 2.1 fusion.133
  238.3 2.1 fusion.131
  240.4 2.1 fusion.130
  242.4 2.6 fusion.58
  246.1 2.2 fusion.89
  248.3 1.9 convolution_bitcast_fusion
  250.2 3.0 pad_maximum_fusion
  253.1 6.6 %copy.47 = f32[768,2048]{1,0:T(8,128)} copy(f32[768,2048]{0,1:T(8,128)} %pad_maximum_fusion) | data formatting | bytes 12582912
  260.9 3.4 fusion.55
  264.2 91.7 %reduce-scatter.4.cloned.1.call-done = f32[48,2048]{1,0:T(8,128)} async-done(((f32[768,2048]{1,0:T(8,128)}), f32[48,2048]{1,0:T(8,128)}) %reduce-scatter.4.cloned.1.call-update) | async-done | bytes 393232
  358.4 2.3 copy.45
  (145 shorter events, 59.9 us)
Async XLA Ops:
  7.2 134.6 %copy-start = (bf16[1024,768]{1,0:T(8,128)(2,1)S(1)}, bf16[1024,768]{1,0:T(8,128)(2,1)}, u32[]{:S(2)}) copy-start(bf16[1024,768]{1,0:T(8,128)(2,1)} %param.17) | copy-start | bytes 4718596
  7.2 12.4 %copy-start.7 = (bf16[1,768,1024]{2,1,0:T(8,128)(2,1)S(1)}, bf16[1,768,1024]{2,1,0:T(8,128)(2,1)}, u32[]{:S(2)}) copy-start(bf16[1,768,1024]{2,1,0:T(8,128)(2,1)} %param.12) | copy-start | bytes 4718596
  24.7 7.5 %copy-start.9 = (s32[16,2]{0,1:T(2,128)S(1)}, s32[16,2]{0,1:T(2,128)}, u32[]{:S(2)}) copy-start(s32[16,2]{0,1:T(2,128)} %param.14) | copy-start | bytes 388
  24.7 7.7 %copy-start.2 = (s32[16]{0:T(128)S(1)}, s32[16]{0:T(128)}, u32[]{:S(2)}) copy-start(s32[16]{0:T(128)} %param.13) | copy-start | bytes 196
  24.7 39.5 %all-to-all-start = ((bf16[16,1,1,48,1024]{4,3,2,1,0:T(8,128)(2,1)}), bf16[16,1,1,48,1024]{4,3,2,1,0:T(8,128)(2,1)S(1)}, u32[]{:S(2)}, u32[]{:S(2)}) async-start(bf16[16,1,1,48,1024]{4,3,2,1,0:T(8,128)(2,1)} %fusion.69), calls=%async_computation | async-start | bytes 3145728 | tf_op jit(solution)/shard_map/all_to_all | solution.py:142
  70.7 9.4 %copy-start.10 = (bf16[1,768,768]{2,1,0:T(8,128)(2,1)S(1)}, bf16[1,768,768]{2,1,0:T(8,128)(2,1)}, u32[]{:S(2)}) copy-start(bf16[1,768,768]{2,1,0:T(8,128)(2,1)} %param.16) | copy-start | bytes 3538948
  70.7 68.7 %all-to-all-start.1 = ((bf16[1,2,16,48,1024]{4,3,1,0,2:T(8,128)(2,1)}), bf16[1,2,16,48,1024]{4,3,1,0,2:T(8,128)(2,1)}, u32[]{:S(2)}, u32[]{:S(2)}) async-start(bf16[1,2,16,48,1024]{4,3,1,0,2:T(8,128)(2,1)} %copy.38), calls=%async_computation.1 | async-start | bytes 6291456 | tf_op jit(solution)/shard_map/all_to_all | solution.py:148
  80.0 275.9 %reduce-scatter.4.cloned.1.call-start = ((), (), s32[]{:S(2)}) async-start(), calls=%async_computation.3 | async-start | bytes 6684672
  82.0 1.5 copy-start.8
  144.6 1.4 copy-start.3
  145.0 1.6 copy-start.12
  147.7 1.6 copy-start.13
  157.6 1.2 copy-start.5
  166.2 2.1 copy-start.6
  168.3 1.2 copy-start.5
  176.8 2.1 copy-start.6
  178.8 1.2 copy-start.5
  187.4 2.1 copy-start.6
  189.4 1.2 copy-start.5
  198.0 2.1 copy-start.6
  200.0 1.2 copy-start.5
  208.6 2.1 copy-start.6
  210.6 1.2 copy-start.5
  219.2 2.1 copy-start.6
  221.2 1.2 copy-start.5
  229.8 2.1 copy-start.6
  231.8 1.2 copy-start.5
  240.4 2.1 copy-start.6
  242.4 2.6 copy-start.4
  242.4 2.6 copy-start.15
  246.1 2.2 copy-start.11
  259.7 1.1 copy-start.14
  355.9 4.8 %copy-start.1 = (bf16[1024,768]{1,0:T(8,128)(2,1)S(1)}, bf16[1024,768]{1,0:T(8,128)(2,1)}, u32[]{:S(2)}) copy-start(bf16[1024,768]{1,0:T(8,128)(2,1)} %param.17) | copy-start | bytes 4718596
Sparse Core Ops, SparseCore 0:
  259.9 95.9 reduce-scatter.3
